TPU v7x, 32 devices: a whole 2x2x4 slice. The times are simulated.
32 devices in a mesh: grp: 4 (over y, x), seq: 8 (over z, core).
Axes of the slice: x: 2, y: 2, z: 4, core: 2. Of those that a mesh axis runs over, the one named last changes fastest.
Arguments:
- queries: bfloat16 [4096, 1024], P(('grp', 'seq')), may hold values from -6 to 6
- keys: bfloat16 [4096, 1024], P(('grp', 'seq')), may hold values from -11 to 11
- values: bfloat16 [4096, 1024], P(('grp', 'seq')), may hold values from -6 to 6
- forget: float32 [4096, 8], P(('grp', 'seq')), may hold values from 0 to 0.5
- beta: float32 [4096, 8], P(('grp', 'seq')), may hold values from 0 to 1
- level_weights: float32 [9, 4096, 8], P(None, ('grp', 'seq')), may hold values from 0.25 to 2
Outputs:
- output: float32 [4096, 1024], P(('grp', 'seq'))
All inputs are finite; a program needn't handle non-finite values.
Results may differ from a plain program's by a relative error of at most 0.0003.
Values sent between devices are 32-bit elements; how exact they have to be, the bound alone decides.
A program may use at most 64 MiB of HBM per device.

v0:
```python
import functools

import jax
import jax.numpy as jnp
from jax import lax
from jax.experimental import pallas as pl
from jax.experimental.pallas import tpu as pltpu
from jax.sharding import PartitionSpec as P

MESH = pl.DeviceIdType.MESH
F32 = jnp.float32
BF16 = jnp.bfloat16
NN = (((1,), (0,)), ((), ()))
NT = (((1,), (1,)), ((), ()))
AUX = 16


def group_bits(heads, n_seq):
    need = heads.bit_length() - 1
    return tuple(range(need - 1)) + (n_seq.bit_length() - 1,)


def dot(a, b, dims=NN):
    return lax.dot_general(a, b, dims, preferred_element_type=F32)


def split(a):
    high = a.astype(BF16)
    return high, (a - high.astype(F32)).astype(BF16)


def mm(a, b, dims=NN):
    ah, al = a
    bh, bl = b
    return dot(ah, bh, dims) + (dot(ah, bl, dims) + dot(al, bh, dims))


def mm_exact(a, b):
    high, low = split(a)
    return dot(high, b) + dot(low, b)


def unit_lower_inverse(lowers, size, row, col):
    apart = row ^ col
    eye = (apart == 0).astype(F32)
    inverses = [eye - jnp.where(apart == 1, low, 0.0) for low in lowers]
    width = 2
    while width < size:
        mask = (apart >= width) & (apart < 2 * width)
        parts = [split(x) for x in inverses]
        blocks = [split(jnp.where(mask, low, 0.0)) for low in lowers]
        left = [split(mm(x, b)) for x, b in zip(parts, blocks)]
        inverses = [x - mm(l, p) for x, l, p in zip(inverses, left, parts)]
        width *= 2
    return inverses


def transitions(blocks, size, dim):
    row = lax.broadcasted_iota(jnp.int32, (size, size), 0)
    col = lax.broadcasted_iota(jnp.int32, (size, size), 1)
    staged = []
    lowers = []
    for block in blocks:
        k, v, aux = block[:size], block[size : 2 * size], block[2 * size :]
        cols = aux.T
        rk = lax.rsqrt(jnp.sum(k * k, -1, keepdims=True) + 1e-06)
        rk_row = jnp.broadcast_to(rk, (size, size)).T
        kb, vb = k.astype(BF16), v.astype(BF16)
        lowers.append(jnp.where(row > col, dot(kb, kb, NT) * rk * rk_row * cols[:, 1:2], 0.0))
        staged.append((kb, vb, rk, rk_row, aux[0:1], aux[1:2], cols))
    inverses = unit_lower_inverse(lowers, size, row, col)
    results = []
    eye = (row == col).astype(F32)
    for inverse, (kb, vb, rk, rk_row, decay_row, beta_row, cols) in zip(inverses, staged):
        update = mm_exact(inverse * (rk_row * beta_row), kb)
        write = mm_exact(inverse * (beta_row / decay_row), vb)
        pair = jnp.concatenate([update, write], 1)
        last = decay_row[:, size - 1 : size]
        moved = mm_exact((pair * rk).T, kb)
        node = jnp.concatenate([last * (eye - moved[:dim]), last * moved[dim:]], 0)
        results.append((node, pair, cols, rk_row))
    return results


def local_reads(q, kb, pair, cols, rk_row, dim):
    size = q.shape[0]
    row = lax.broadcasted_iota(jnp.int32, (size, size), 0)
    col = lax.broadcasted_iota(jnp.int32, (size, size), 1)
    rq = lax.rsqrt(jnp.sum(q * q, -1, keepdims=True) + 1e-06)
    scores = jnp.where(row >= col, dot(q.astype(BF16), kb, NT) * rq * rk_row, 0.0)
    seen = mm(split(scores), split(pair))
    decay_col = cols[:, 0:1]
    return decay_col * (q * rq - seen[:, :dim]), decay_col * seen[:, dim:] * cols[:, 2:3]


def join(lower, upper, dim):
    both = mm(split(lower), split(upper[:dim]))
    return jnp.concatenate([both[:dim], both[dim:] + upper[dim:]], 0)


def kernel(n_grp, n_seq, heads, *refs):
    q_ref, k_ref, v_ref, aux_ref, out_ref = refs[:5]
    kv_out, q_out, kv_in, q_in, pairs, cols, rks, reach, acc, joined = refs[5:15]
    bits = group_bits(heads, n_seq)
    low_levels = len(bits) - 1
    cross = bits[-1]
    total_bits = (n_grp * n_seq).bit_length() - 1
    middle = list(range(low_levels, cross))
    upward = list(range(cross + 1, total_bits))
    refs = refs[15:]
    trees, refs = refs[:low_levels], refs[low_levels:]
    n_mid, n_up = len(middle), len(upward)
    mid_out, mid_in = refs[:n_mid], refs[n_mid : 2 * n_mid]
    refs = refs[2 * n_mid :]
    up_out, up_in = refs[:n_up], refs[n_up : 2 * n_up]
    s_kv, r_kv, s_q, r_q, s_mid, r_mid, s_up, r_up, s_out, r_out = refs[2 * n_up :]
    size = q_ref.shape[0]
    dim = q_ref.shape[1] // heads
    half = heads // 2
    pos = lax.axis_index("grp") * n_seq + lax.axis_index("seq")

    def bit_of(number, l):
        return (number // (1 << l)) % 2

    me = sum(bit_of(pos, l) * (1 << m) for m, l in enumerate(bits))
    base = pos - sum(bit_of(pos, l) * (1 << l) for l in bits)
    side, place = me // half, me % half

    def where_is(number):
        return (number // n_seq, number % n_seq)

    def member(i):
        return where_is(base + sum(bit_of(i, m) * (1 << l) for m, l in enumerate(bits)))

    def partner(l):
        return where_is(pos + (1 - 2 * bit_of(pos, l)) * (1 << l))

    def slot(rank, sign):
        far, r = rank // half, rank % half
        spot = (place + half + sign * 2 * (r // 2)) % half
        if r % 2:
            spot = spot + 1 - 2 * (spot % 2)
        which = 1 - side if far else side
        return which * half + spot

    def columns(i):
        return pl.ds(pl.multiple_of(i * dim, dim), dim)

    barrier = pltpu.get_barrier_semaphore()
    for rank in range(1, heads):
        pl.semaphore_signal(
            barrier, inc=1, device_id=member(slot(rank, 1)), device_id_type=MESH
        )
    for l in middle + upward:
        pl.semaphore_signal(barrier, inc=1, device_id=partner(l), device_id_type=MESH)
    for i in range(heads):
        part = slice(i * dim, (i + 1) * dim)
        kv_out[i, :size] = k_ref[:, part].astype(F32)
        kv_out[i, size : 2 * size] = v_ref[:, part].astype(F32)
        kv_out[i, 2 * size :] = aux_ref[i]
        q_out[i] = q_ref[:, part].astype(F32)
    pl.semaphore_wait(barrier, heads - 1 + n_mid + n_up)

    def remote(source, target, send, receive, device):
        copy = pltpu.make_async_remote_copy(
            src_ref=source,
            dst_ref=target,
            send_sem=send,
            recv_sem=receive,
            device_id=device,
            device_id_type=MESH,
        )
        return copy

    pending = []
    kv_copies, q_copies = {}, {}
    for out, into, send, receive, copies in (
        (kv_out, kv_in, s_kv, r_kv, kv_copies),
        (q_out, q_in, s_q, r_q, q_copies),
    ):
        for rank in range(1, heads):
            i = slot(rank, 1)
            copies[rank] = remote(
                out.at[i], into.at[me], send.at[rank], receive.at[rank], member(i)
            )
    for copy in kv_copies.values():
        copy.start()
    pending += list(kv_copies.values()) + list(q_copies.values())

    def send_queries(ranks):
        for rank in ranks:
            if 0 < rank < heads:
                q_copies[rank].start()

    send_queries((1, half, half + 1))
    kv_in[me] = kv_out[me]
    q_in[me] = q_out[me]

    mid_copies = [{} for l in middle]

    def send_mid(m, which):
        copy = remote(
            mid_out[m].at[which],
            mid_in[m].at[which],
            s_mid.at[m, which],
            r_mid.at[m, which],
            partner(middle[m]),
        )
        copy.start()
        pending.append(copy)
        return copy

    first_mid = []
    for far in range(2):
        which = 1 - side if far else side
        for first in range(0, half, 2):
            slots = []
            for rank in (far * half + first, far * half + first + 1):
                if rank:
                    kv_copies[rank].wait_recv()
                slots.append(slot(rank, -1))
            done = transitions([kv_in[i] for i in slots], size, dim)
            for i, (node, pair, col, rk_row) in zip(slots, done):
                trees[0][i] = node
                pairs[i] = pair
                cols[i] = col
                rks[i] = rk_row[:8]
        for m in range(low_levels):
            count = half >> (m + 1)
            for j in range(count):
                lower = trees[m][which * 2 * count + 2 * j]
                upper = trees[m][which * 2 * count + 2 * j + 1]
                node = join(lower, upper, dim)
                if m + 1 < low_levels:
                    trees[m + 1][which * count + j] = node
                else:
                    mid_out[0][which] = node
        first_mid.append(send_mid(0, which))
        send_queries(range(far * half + 2, far * half + half))

    def read(j, lower, l, gate=None):
        seen = mm(split(reach[j]), lower, NT)
        far = cols[j, :, 3 + l : 4 + l] * seen[:, seen.shape[1] - dim :]
        acc[j] += far if gate is None else jnp.where(gate, far, 0.0)
        if seen.shape[1] > dim:
            new = seen[:, :dim]
            reach[j] = new if gate is None else jnp.where(gate, new, reach[j])

    for first in range(0, heads, 2):
        for rank in (first, first + 1):
            if rank:
                q_copies[rank].wait_recv()
            i = slot(rank, -1)
            rk_row = jnp.broadcast_to(rks[i][:1], (size, size))
            near = local_reads(
                q_in[i], kv_in[i, :size, :].astype(BF16), pairs[i], cols[i], rk_row, dim
            )
            reach[i], acc[i] = near
    for m in range(low_levels):
        for key in range(0, heads, 2 << m):
            lower = split(trees[m][key >> m])
            for j in range(key + (1 << m), key + (2 << m)):
                read(j, lower, m)

    copies = first_mid
    for m, l in enumerate(middle):
        upper_side = bit_of(pos, l) == 1
        following = []
        for far in range(2):
            which = 1 - side if far else side
            copies[far].wait_recv()
            peer, mine = mid_in[m][which], mid_out[m][which]
            lower = jnp.where(upper_side, peer, mine)
            upper = jnp.where(upper_side, mine, peer)
            node = join(lower, upper, dim)
            if m + 1 < n_mid:
                mid_out[m + 1][which] = node
                following.append(send_mid(m + 1, which))
            else:
                joined[which] = node
        copies = following

    node = join(joined[0], joined[1], dim)

    def send_up(m):
        copy = remote(up_out[m], up_in[m], s_up.at[m], r_up.at[m], partner(upward[m]))
        copy.start()
        pending.append(copy)
        return copy

    up_out[0][...] = node[dim:] if n_up == 1 else node
    copy = send_up(0)
    for m, l in enumerate(middle):
        gate = bit_of(pos, l) == 1
        for which in range(2):
            lower = split(mid_in[m][which])
            for j in range(which * half, (which + 1) * half):
                read(j, lower, l, gate)
    lower = split(joined[0])
    for j in range(half, heads):
        read(j, lower, cross)
    for m, l in enumerate(upward):
        gate = bit_of(pos, l) == 1
        copy.wait_recv()
        peer = up_in[m][...]
        if m + 1 < n_up:
            mine = up_out[m][...]
            node = join(jnp.where(gate, peer, mine), jnp.where(gate, mine, peer), dim)
            up_out[m + 1][...] = node[dim:] if m + 2 == n_up else node
            copy = send_up(m + 1)
        lower = split(peer)
        for rank in range(heads - 1, -1, -1):
            if m + 1 < n_up:
                read(rank, lower, l, gate)
                continue
            i = slot(rank, 1)
            read(i, lower, l, gate)
            if rank == 0:
                out_ref[:, columns(me)] = acc[me]
                continue
            back = remote(
                acc.at[i], out_ref.at[:, columns(me)], s_out.at[rank], r_out.at[rank], member(i)
            )
            back.start()
            pending.append(back)
    for rank in range(1, heads):
        source = slot(rank, -1)
        remote(
            acc.at[source],
            out_ref.at[:, columns(source)],
            s_out.at[rank],
            r_out.at[rank],
            member(source),
        ).wait_recv()
    for copy in pending:
        copy.wait_send()


def on_device(n_grp, n_seq, queries, keys, values, forget, beta, level_weights):
    size = queries.shape[0]
    heads = forget.shape[1]
    dim = queries.shape[1] // heads
    levels = level_weights.shape[0]
    bits = group_bits(heads, n_seq)
    total_bits = (n_grp * n_seq).bit_length() - 1
    low_levels, cross = len(bits) - 1, bits[-1]
    n_mid, n_up = cross - low_levels, total_bits - cross - 1
    decays = jnp.exp(-jnp.cumsum(forget, 0)).T
    small = jnp.concatenate(
        [
            decays[:, None],
            beta.T[:, None],
            jnp.transpose(level_weights, (2, 0, 1)),
            jnp.zeros((heads, AUX - 2 - levels, size), F32),
        ],
        1,
    )
    mids = [pltpu.VMEM((2, 2 * dim, dim), F32)] * n_mid
    ups = [pltpu.VMEM((2 * dim, dim), F32)] * (n_up - 1) + [pltpu.VMEM((dim, dim), F32)]
    dma = pltpu.SemaphoreType.DMA
    return pl.pallas_call(
        functools.partial(kernel, n_grp, n_seq, heads),
        out_shape=pltpu.VMEM((size, heads * dim), F32),
        in_specs=[pl.BlockSpec(memory_space=pltpu.VMEM)] * 4,
        out_specs=pl.BlockSpec(memory_space=pltpu.VMEM),
        scratch_shapes=[
            pltpu.VMEM((heads, 2 * size + AUX, dim), F32),
            pltpu.VMEM((heads, size, dim), F32),
            pltpu.VMEM((heads, 2 * size + AUX, dim), F32),
            pltpu.VMEM((heads, size, dim), F32),
            pltpu.VMEM((heads, size, 2 * dim), F32),
            pltpu.VMEM((heads, size, AUX), F32),
            pltpu.VMEM((heads, 8, size), F32),
            pltpu.VMEM((heads, size, dim), F32),
            pltpu.VMEM((heads, size, dim), F32),
            pltpu.VMEM((2, 2 * dim, dim), F32),
        ]
        + [pltpu.VMEM((heads >> m, 2 * dim, dim), F32) for m in range(low_levels)]
        + mids
        + mids
        + ups
        + ups
        + [dma((heads,))] * 4
        + [dma((n_mid, 2))] * 2
        + [dma((n_up,))] * 2
        + [dma((heads,))] * 2,
        compiler_params=pltpu.CompilerParams(collective_id=0, has_side_effects=True),
    )(queries, keys, values, small)


def solution(mesh):
    both = P(("grp", "seq"), None)
    return jax.shard_map(
        functools.partial(on_device, mesh.shape["grp"], mesh.shape["seq"]),
        mesh=mesh,
        in_specs=(both, both, both, both, both, P(None, ("grp", "seq"), None)),
        out_specs=both,
        check_vma=False,
    )
```

profile of v0, /device:TPU:0, one launch (start us, length us, event | category | flops | bytes accessed | tf_op | source)
XLA Modules:
  0.0 47.9 jit_solution(18281852953725418736)
XLA Ops:
  0.0 0.0 copy-start.1
  0.0 0.1 pad.3.clone
  0.1 0.6 %copy-done.1 = f32[128,8]{0,1:T(8,128)S(1)} copy-done((f32[128,8]{0,1:T(8,128)S(1)}, f32[128,8]{0,1:T(8,128)}, u32[]{:S(2)}) %copy-start.1) | copy-done | bytes 4120
  0.7 0.1 copy.7
  0.8 0.2 reduce_window_sum.11
  1.0 0.0 copy-start
  1.0 0.7 %copy-done = f32[9,128,8]{1,2,0:T(8,128)S(1)} copy-done((f32[9,128,8]{1,2,0:T(8,128)S(1)}, f32[9,128,8]{1,2,0:T(8,128)}, u32[]{:S(2)}) %copy-start) | copy-done | bytes 36888
  1.7 0.0 copy-start.2
  1.7 0.7 %copy-done.2 = f32[128,8]{0,1:T(8,128)S(1)} copy-done((f32[128,8]{0,1:T(8,128)S(1)}, f32[128,8]{0,1:T(8,128)}, u32[]{:S(2)}) %copy-start.2) | copy-done | bytes 4120
  2.4 0.7 %maximum_maximum_fusion.refs_3_ = f32[8,16,128]{2,1,0:T(8,128)} fusion(f32[8,9,128]{2,1,0:T(8,128)S(1)} %bitcast.9, f32[8,1,128]{2,1,0:T(1,128)S(1)} %bitcast.11, f32[8,1,128]{2,1,0:T(1,128)S(1)} %bitcast.10, f32[16]{0:T(128)S(1)} %pad.3.clone), kind=kLoop, calls=%fused_computation | loop fusion | flops 49152 | bytes 110656 | tf_op jit(solution)/shard_map/concatenate | solution.py:349
  3.1 44.0 %shard_map.64 = f32[128,1024]{1,0:T(8,128)S(1)} custom-call(bf16[128,1024]{1,0:T(8,128)(2,1)} %refs_0_.1, bf16[128,1024]{1,0:T(8,128)(2,1)} %refs_1_.1, bf16[128,1024]{1,0:T(8,128)(2,1)} %refs_2_.1, f32[8,16,128]{2,1,0:T(8,128)} %maximum_maximum_fusion.refs_3_), custom_call_target="tpu_custom_call" | custom-call | tf_op jit(solution)/shard_map/pallas_call | solution.py:361
  47.1 0.8 %copy.13 = f32[128,1024]{1,0:T(8,128)} copy(f32[128,1024]{1,0:T(8,128)S(1)} %shard_map.64) | data formatting | bytes 1048576
  (4 shorter events, 0.1 us)
Async XLA Ops:
  0.0 0.7 %copy-start.1 = (f32[128,8]{0,1:T(8,128)S(1)}, f32[128,8]{0,1:T(8,128)}, u32[]{:S(2)}) copy-start(f32[128,8]{0,1:T(8,128)} %param.9) | copy-start | bytes 12292
  1.0 0.8 %copy-start = (f32[9,128,8]{1,2,0:T(8,128)S(1)}, f32[9,128,8]{1,2,0:T(8,128)}, u32[]{:S(2)}) copy-start(f32[9,128,8]{1,2,0:T(8,128)} %param.11) | copy-start | bytes 110596
  1.7 0.7 %copy-start.2 = (f32[128,8]{0,1:T(8,128)S(1)}, f32[128,8]{0,1:T(8,128)}, u32[]{:S(2)}) copy-start(f32[128,8]{0,1:T(8,128)} %param.10) | copy-start | bytes 12292
where the time goes:
time: 48.2 us; the launch traced here: 47.9 us
  Pallas kernels  44 us (91%)
  local copies, waits for them, and re-layouts  3.02 us (6%)
  other arithmetic  0.88 us (2%)
    pallas_call x1, Pallas kernels, on_device(): pl.pallas_call(functools.partial(kernel, n_grp, n_seq, heads), out_shape=...  44 us
    unnamed x9, local copies, waits for them, and re-layouts  2.9 us

commit v1 on v0

v1 whole, which is shorter than its diff:
```python
import functools

import jax
import jax.numpy as jnp
from jax import lax
from jax.experimental import pallas as pl
from jax.experimental.pallas import tpu as pltpu
from jax.sharding import PartitionSpec as P

MESH = pl.DeviceIdType.MESH
F32 = jnp.float32
BF16 = jnp.bfloat16
NN = (((1,), (0,)), ((), ()))
NT = (((1,), (1,)), ((), ()))
AUX = 16
TILE = 16
EPS = 1e-06


def dot(a, b, dims=NN):
    return lax.dot_general(a, b, dims, preferred_element_type=F32)


def split(a):
    high = a.astype(BF16)
    return high, (a - high.astype(F32)).astype(BF16)


def mm(a, b):
    ah, al = a
    bh, bl = b
    return dot(ah, bh) + (dot(ah, bl) + dot(al, bh))


def mm_square(a, b):
    ah, al = a
    bh, bl = b
    right = jnp.concatenate(
        [jnp.concatenate([bh, bl], 1), jnp.concatenate([bh, jnp.zeros_like(bl)], 1)], 0
    )
    both = dot(jnp.concatenate([ah, al], 1), right)
    width = bh.shape[1]
    return both[:, :width] + both[:, width:]


def mm_exact(a, b):
    return dot(jnp.concatenate(a, 1), jnp.concatenate([b, b], 0))


def tile_inverse(low, size):
    lane = lax.broadcasted_iota(jnp.int32, (TILE, size), 1)
    sub = lax.broadcasted_iota(jnp.int32, (TILE, size), 0)
    tile = lane // TILE
    packed = low[:TILE]
    for g in range(1, size // TILE):
        packed = jnp.where(tile == g, low[g * TILE : (g + 1) * TILE], packed)
    inner = lane - tile * TILE
    packed = jnp.where(sub > inner, packed, 0.0)
    x = jnp.where(sub == inner, 1.0, 0.0)
    for c in range(TILE - 1):
        column = jnp.take_along_axis(packed, tile * TILE + c, axis=1)
        x = x - column * x[c : c + 1]
    return jnp.concatenate(
        [jnp.where(tile == g, x, 0.0) for g in range(size // TILE)], 0
    )


def unit_lower_inverse(lowers, size, row, col):
    apart = row ^ col
    inverses = [tile_inverse(low, size) for low in lowers]
    width = TILE
    while width < size:
        mask = (apart >= width) & (apart < 2 * width)
        parts = [split(x) for x in inverses]
        blocks = [split(jnp.where(mask, low, 0.0)) for low in lowers]
        left = [split(mm_square(x, b)) for x, b in zip(parts, blocks)]
        inverses = [x - mm_square(l, p) for x, l, p in zip(inverses, left, parts)]
        width *= 2
    return inverses


def transitions(blocks, size, dim):
    row = lax.broadcasted_iota(jnp.int32, (size, size), 0)
    col = lax.broadcasted_iota(jnp.int32, (size, size), 1)
    aux_row = lax.broadcasted_iota(jnp.int32, (AUX, size), 0)
    staged, lowers = [], []
    for kb, vb, aux in blocks:
        gram = dot(kb, kb, NT)
        norm = jnp.sum(jnp.where(row == col, gram, 0.0), 0, keepdims=True) + EPS
        rk = lax.rsqrt(norm)
        gain = aux[1:2] * (rk * rk)
        decay = aux[0:1]
        cols = jnp.where(aux_row == AUX - 1, gain, aux).T
        lowers.append(jnp.where(row > col, gram * gain, 0.0))
        staged.append((kb, vb, gain, norm * rk / decay, decay[:, size - 1 : size], cols))
    inverses = unit_lower_inverse(lowers, size, row, col)
    eye = (row == col).astype(F32)
    results = []
    for inverse, (kb, vb, gain, unscale, last, cols) in zip(inverses, staged):
        y = mm_exact(split(inverse), kb)
        z = mm_exact(split(inverse * unscale), vb)
        pair = jnp.concatenate([y, z], 1)
        kt = kb.astype(F32).T.astype(BF16)
        moved = dot(
            jnp.concatenate([kt, kt], 1),
            jnp.concatenate(split(pair * cols[:, AUX - 1 : AUX]), 0),
        )
        node = jnp.concatenate([last * (eye - moved[:, :dim]), last * moved[:, dim:]], 1)
        results.append((node, pair, cols, gain))
    return results


def local_reads(qb, kb, pair, cols, gain):
    size = qb.shape[0]
    dim = qb.shape[1]
    row = lax.broadcasted_iota(jnp.int32, (size, size), 0)
    col = lax.broadcasted_iota(jnp.int32, (size, size), 1)
    q = qb.astype(F32)
    scale = lax.rsqrt(jnp.sum(q * q, -1, keepdims=True) + EPS) * cols[:, 0:1]
    scores = jnp.where(row >= col, dot(qb, kb, NT) * gain, 0.0)
    seen = mm(split(scores), split(pair))
    return scale * (q - seen[:, :dim]), (scale * cols[:, 2:3]) * seen[:, dim:]


def join(lower, upper, dim):
    both = mm(split(upper[:, :dim]), split(lower))
    return jnp.concatenate([both[:, :dim], both[:, dim:] + upper[:, dim:]], 1)


def kernel(n_grp, n_seq, heads, *refs):
    q_ref, k_ref, v_ref, f_ref, b_ref, w_ref, out_ref = refs[:7]
    (
        aux,
        kv_out,
        q_out,
        kv_in,
        q_in,
        pairs,
        colb,
        gains,
        blocks,
        nodes,
        node_in,
        r_out,
        r_in,
        colr,
        near,
        near_in,
        far,
        far_in,
        joined,
    ) = refs[7:26]
    refs = refs[26:]
    total_bits = (n_grp * n_seq).bit_length() - 1
    cross = n_seq.bit_length() - 1
    middle = list(range(2, cross))
    upward = list(range(cross + 1, total_bits))
    n_mid, n_up = len(middle), len(upward)
    mids, refs = refs[:n_mid], refs[n_mid:]
    up_out, up_in, refs = refs[:n_up], refs[n_up : 2 * n_up], refs[2 * n_up :]
    (
        s_kv,
        r_kv,
        s_q,
        r_q,
        s_node,
        r_node,
        s_r,
        r_r,
        s_mid,
        r_mid,
        s_up,
        r_up,
        s_near,
        r_near,
        s_far,
        r_far,
    ) = refs
    size = q_ref.shape[0]
    dim = q_ref.shape[1] // heads
    slots = heads // 2
    pos = lax.axis_index("grp") * n_seq + lax.axis_index("seq")

    def bit_of(l):
        return (pos // (1 << l)) % 2

    core, zl, xx = bit_of(0), bit_of(1), bit_of(cross)
    base = pos - core - 2 * zl - xx * (1 << cross)
    place = 2 * xx + zl

    def where_is(number):
        return (number // n_seq, number % n_seq)

    def place_of(m):
        return 2 * (1 - xx if m & 2 else xx) + (1 - zl if m & 1 else zl)

    def member(m, c):
        z = 1 - zl if m & 1 else zl
        x = 1 - xx if m & 2 else xx
        return where_is(base + c + 2 * z + x * (1 << cross))

    def partner(l):
        return where_is(pos + (1 - 2 * bit_of(l)) * (1 << l))

    def columns(i):
        return pl.ds(pl.multiple_of(i * dim, dim), dim)

    def remote(source, target, send, receive, device):
        return pltpu.make_async_remote_copy(
            src_ref=source,
            dst_ref=target,
            send_sem=send,
            recv_sem=receive,
            device_id=device,
            device_id_type=MESH,
        )

    other = 1 - core
    barrier = pltpu.get_barrier_semaphore()
    for m in range(4):
        for c in (core, other):
            if m or c is other:
                pl.semaphore_signal(barrier, inc=1, device_id=member(m, c), device_id_type=MESH)
    for l in middle + upward:
        pl.semaphore_signal(barrier, inc=1, device_id=partner(l), device_id_type=MESH)

    total = f_ref[...]
    lane = lax.broadcasted_iota(jnp.int32, total.shape, 1)
    step = 1
    while step < size:
        total = total + jnp.where(lane >= step, pltpu.roll(total, step, 1), 0.0)
        step *= 2
    decay = jnp.exp(-total)
    aux[...] = jnp.zeros_like(aux)
    levels = w_ref.shape[0]
    for h in range(heads):
        aux[h, 0:1] = decay[h : h + 1]
        aux[h, 1:2] = b_ref[h : h + 1]
        for l in range(levels):
            aux[h, 2 + l : 3 + l] = w_ref[l, h : h + 1]

    order = (0, 3, 1, 2)
    for j in order:
        h = other * slots + j
        kv_out[j, :size] = k_ref[:, columns(h)].astype(F32)
        kv_out[j, size : 2 * size] = v_ref[:, columns(h)].astype(F32)
        kv_out[j, 2 * size :] = aux[h]
        q_out[j] = q_ref[:, columns(h)].astype(F32)
    pl.semaphore_wait(barrier, 7 + n_mid + n_up)

    pending = []
    kv_copies, q_copies = {}, {}
    for j in order:
        kv_copies[j] = remote(
            kv_out.at[j], kv_in.at[j], s_kv.at[j], r_kv.at[j], member(0, other)
        )
        q_copies[j] = remote(q_out.at[j], q_in.at[j], s_q.at[j], r_q.at[j], member(0, other))
    for copies in (kv_copies, q_copies):
        for j in order:
            copies[j].start()
            pending.append(copies[j])

    def own_block(j):
        h = core * slots + j
        return k_ref[:, columns(h)], v_ref[:, columns(h)], aux[h]

    def other_block(j):
        return (
            kv_in[j, :size].astype(BF16),
            kv_in[j, size : 2 * size].astype(BF16),
            kv_in[j, 2 * size :],
        )

    def solve(work):
        done = transitions(
            [own_block(j) if e == 0 else other_block(j) for j, e in work], size, dim
        )
        for (j, e), (node, pair, cols, gain) in zip(work, done):
            blocks[other if e else core, j] = node
            pairs[e, j] = pair
            colb[e, j] = cols
            gains[e, j] = jnp.broadcast_to(gain, (8, size))

    node_copies, r_copies = {}, {}
    for m in range(1, 4):
        node_copies[m] = remote(
            nodes.at[place_of(m)],
            node_in.at[place],
            s_node.at[m],
            r_node.at[m],
            member(m, core),
        )
        r_copies[m] = [
            remote(
                r_out.at[place_of(m), s],
                r_in.at[place, s],
                s_r.at[2 * m + s],
                r_r.at[2 * m + s],
                member(m, core),
            )
            for s in range(2)
        ]
        pending.append(node_copies[m])
        pending += r_copies[m]

    def send_group(group, start):
        diagonal = (zl == xx) if group == 0 else (zl != xx)
        straight = (zl != xx) if group == 0 else (zl == xx)

        @pl.when(diagonal)
        def _():
            start(3)

        @pl.when(straight)
        def _():
            start(1)
            start(2)

    def merge(group):
        for j in group:
            nodes[j] = join(blocks[0, j], blocks[1, j], dim)

    def send_nodes(m):
        node_copies[m].start()

    def send_reads(m):
        for copy in r_copies[m]:
            copy.start()

    groups = ((0, 3), (1, 2))
    solve([(j, 0) for j in groups[0]])
    for j in groups[0]:
        kv_copies[j].wait_recv()
    solve([(j, 1) for j in groups[0]] + [(j, 0) for j in groups[1]])
    merge(groups[0])
    send_group(0, send_nodes)
    for j in groups[1]:
        kv_copies[j].wait_recv()
    solve([(j, 1) for j in groups[1]])
    merge(groups[1])
    send_group(1, send_nodes)

    def reads(group):
        for j in group:
            q_copies[j].wait_recv()
        for j in group:
            h = core * slots + j
            for e in range(2):
                if e == 0:
                    qb, kb, _ = q_ref[:, columns(h)], k_ref[:, columns(h)], None
                else:
                    qb, kb = q_in[j].astype(BF16), kv_in[j, :size].astype(BF16)
                s = other if e else core
                r, inside = local_reads(qb, kb, pairs[e, j], colb[e, j], gains[e, j, :1])
                r_out[j, s, :size] = r
                r_out[j, s, size:] = kv_in[j, 2 * size :] if e else aux[h]
                near[j, s] = inside
        for j in group:
            seen = mm(split(r_out[j, 1, :size]), split(blocks[0, j]))
            weight = jnp.where(core == 1, colb[0, j], colb[1, j])[:, 3:4]
            r_out[j, 1, :size] = seen[:, :dim]
            near[j, 1] += weight * seen[:, dim:]

    reads(groups[0])

    node_in[place] = nodes[place]
    for m in range(1, 4):
        node_copies[m].wait_recv()

    def send_mid(m, x):
        mine = bit_of(middle[m])
        copy = remote(
            mids[m].at[x, mine],
            mids[m].at[x, mine],
            s_mid.at[m, x],
            r_mid.at[m, x],
            partner(middle[m]),
        )
        copy.start()
        pending.append(copy)

    def wait_mid(m, x):
        theirs = 1 - bit_of(middle[m])
        remote(
            mids[m].at[x, theirs],
            mids[m].at[x, theirs],
            s_mid.at[m, x],
            r_mid.at[m, x],
            partner(middle[m]),
        ).wait_recv()

    for x in range(2):
        mids[0][x, bit_of(middle[0])] = join(node_in[2 * x], node_in[2 * x + 1], dim)
    for x in range(2):
        send_mid(0, x)

    send_group(0, send_reads)
    reads(groups[1])
    send_group(1, send_reads)
    near_copies = []
    for j in range(slots):
        copy = remote(
            near.at[j, other], near_in.at[j], s_near.at[j], r_near.at[j], member(0, other)
        )
        copy.start()
        near_copies.append(copy)
        pending.append(copy)
    for s in range(2):
        r_in[place, s] = r_out[place, s]

    for m in range(n_mid):
        for x in range(2):
            wait_mid(m, x)
        for x in range(2):
            node = join(mids[m][x, 0], mids[m][x, 1], dim)
            if m + 1 < n_mid:
                mids[m + 1][x, bit_of(middle[m + 1])] = node
            else:
                joined[x] = node
        if m + 1 < n_mid:
            for x in range(2):
                send_mid(m + 1, x)
    whole = join(joined[0], joined[1], dim)

    def send_up(m):
        copy = remote(up_out[m], up_in[m], s_up.at[m], r_up.at[m], partner(upward[m]))
        copy.start()
        pending.append(copy)
        return copy

    up_out[0][...] = whole[:, dim:] if n_up == 1 else whole
    copy = send_up(0)

    for m in range(1, 4):
        for c in r_copies[m]:
            c.wait_recv()
    for i in range(4):
        for s in range(2):
            colr[i, s] = r_in[i, s, size:].T

    def read(items, lower, l, gate=None, fresh=False):
        rows = jnp.concatenate([r_in[i, s, :size] for i, s in items], 0)
        seen = mm(split(rows), lower)
        for n, (i, s) in enumerate(items):
            part = seen[n * size : (n + 1) * size]
            value = colr[i, s][:, 3 + l : 4 + l] * part[:, part.shape[1] - dim :]
            if gate is not None:
                value = jnp.where(gate, value, 0.0)
            far[i, s] = value if fresh else far[i, s] + value
            if part.shape[1] > dim:
                new = part[:, :dim]
                r_in[i, s, :size] = (
                    new if gate is None else jnp.where(gate, new, r_in[i, s, :size])
                )

    for x in range(2):
        for s in range(2):
            far[2 * x, s] = jnp.zeros((size, dim), F32)
        read([(2 * x + 1, 0), (2 * x + 1, 1)], split(node_in[2 * x]), 1, fresh=True)
    for m, l in enumerate(middle):
        gate = bit_of(l) == 1
        for x in range(2):
            items = [(2 * x + z, s) for z in range(2) for s in range(2)]
            read(items, split(mids[m][x, 0]), l, gate)
    read([(2 + z, s) for z in range(2) for s in range(2)], split(joined[0]), cross)

    everyone = [(i, s) for i in range(4) for s in range(2)]
    for m, l in enumerate(upward):
        gate = bit_of(l) == 1
        copy.wait_recv()
        if m + 1 < n_up:
            peer, mine = up_in[m][...], up_out[m][...]
            node = join(jnp.where(gate, peer, mine), jnp.where(gate, mine, peer), dim)
            up_out[m + 1][...] = node[:, dim:] if m + 2 == n_up else node
            copy = send_up(m + 1)
            read(everyone, split(peer), l, gate)

    gate = bit_of(upward[-1]) == 1
    lower = split(up_in[-1][...])
    far_copies = {}
    for m in (3, 2, 1, 0):
        i = place_of(m)
        for e in (1, 0):
            s = other if e else core
            seen = mm(split(r_in[i, s, :size]), lower)
            weight = colr[i, s][:, 3 + upward[-1] : 4 + upward[-1]]
            far[i, s] += jnp.where(gate, weight * seen, 0.0)
            if m == 0 and e == 0:
                far_in[core * slots + place] = far[place, core]
                continue
            far_copies[m, e] = remote(
                far.at[i, s],
                far_in.at[core * slots + place],
                s_far.at[2 * m + e],
                r_far.at[2 * m + e],
                member(m, s),
            )
            far_copies[m, e].start()
            pending.append(far_copies[m, e])

    for copy in near_copies:
        copy.wait_recv()
    for m in range(4):
        for e in range(2):
            c = other if e else core
            j = place_of(m)
            h = c * slots + j
            if m or e:
                remote(
                    far.at[j, core],
                    far_in.at[h],
                    s_far.at[2 * m + e],
                    r_far.at[2 * m + e],
                    member(m, c),
                ).wait_recv()
            mine = near_in[j] if e else near[j, core]
            out_ref[:, columns(h)] = mine + far_in[h]
    for copy in pending:
        copy.wait_send()


def on_device(n_grp, n_seq, queries, keys, values, forget, beta, level_weights):
    size = queries.shape[0]
    heads = forget.shape[1]
    dim = queries.shape[1] // heads
    slots = heads // 2
    total_bits = (n_grp * n_seq).bit_length() - 1
    cross = n_seq.bit_length() - 1
    n_mid, n_up = cross - 2, total_bits - cross - 1
    node = (dim, 2 * dim)
    dma = pltpu.SemaphoreType.DMA

    def vmem(*shape):
        return pltpu.VMEM(shape, F32)

    ups = [vmem(*node)] * (n_up - 1) + [vmem(dim, dim)]
    return pl.pallas_call(
        functools.partial(kernel, n_grp, n_seq, heads),
        out_shape=pltpu.VMEM((size, heads * dim), F32),
        in_specs=[pl.BlockSpec(memory_space=pltpu.VMEM)] * 6,
        out_specs=pl.BlockSpec(memory_space=pltpu.VMEM),
        scratch_shapes=[
            vmem(heads, AUX, size),
            vmem(slots, 2 * size + AUX, dim),
            vmem(slots, size, dim),
            vmem(slots, 2 * size + AUX, dim),
            vmem(slots, size, dim),
            vmem(2, slots, size, 2 * dim),
            vmem(2, slots, size, AUX),
            vmem(2, slots, 8, size),
            vmem(2, slots, *node),
            vmem(slots, *node),
            vmem(4, *node),
            vmem(slots, 2, size + AUX, dim),
            vmem(4, 2, size + AUX, dim),
            vmem(4, 2, size, AUX),
            vmem(slots, 2, size, dim),
            vmem(slots, size, dim),
            vmem(4, 2, size, dim),
            vmem(heads, size, dim),
            vmem(2, *node),
        ]
        + [vmem(2, 2, *node)] * n_mid
        + ups
        + ups
        + [dma((slots,))] * 4
        + [dma((4,))] * 2
        + [dma((8,))] * 2
        + [dma((n_mid, 2))] * 2
        + [dma((n_up,))] * 2
        + [dma((slots,))] * 2
        + [dma((8,))] * 2,
        compiler_params=pltpu.CompilerParams(collective_id=0, has_side_effects=True),
    )(
        queries,
        keys,
        values,
        forget.T,
        beta.T,
        jnp.transpose(level_weights, (0, 2, 1)),
    )


def solution(mesh):
    both = P(("grp", "seq"), None)
    return jax.shard_map(
        functools.partial(on_device, mesh.shape["grp"], mesh.shape["seq"]),
        mesh=mesh,
        in_specs=(both, both, both, both, both, P(None, ("grp", "seq"), None)),
        out_specs=both,
        check_vma=False,
    )
```

time: 48.2 us -> 42.3 us (0.88)
  Pallas kernels: 44 us -> 41.3 us
  local copies, waits for them, and re-layouts: 3.02 us -> 0.8 us
  other arithmetic: 0.88 us -> 0 us
    pallas_call x1, Pallas kernels: 44 us -> 41.3 us  [on_device(): pl.pallas_call(functools.partial(kernel, n_grp, n_seq, heads), out_shape=...]
    unnamed x9 -> x1, local copies, waits for them, and re-layouts: 2.9 us -> 0.8 us
    concatenate x1 -> x0, other arithmetic: 0.7 us -> none  [on_device(): jnp.concatenate([decays[:, None], beta.T[:, None], jnp.transpose(level_we...]
where the time goes in v1:
time: 42.3 us; the launch traced here: 42.1 us
  Pallas kernels  41.3 us (98%)
  local copies, waits for them, and re-layouts  0.8 us (2%)
    pallas_call x1, Pallas kernels, on_device(): pl.pallas_call(functools.partial(kernel, n_grp, n_seq, heads), out_shape=...  41.3 us

profile of v1, /device:TPU:0, one launch (start us, length us, event | category | flops | bytes accessed | tf_op | source)
XLA Modules:
  0.0 42.1 jit_solution(17037287968807876675)
XLA Ops:
  0.0 41.3 %shard_map.64 = f32[128,1024]{1,0:T(8,128)S(1)} custom-call(bf16[128,1024]{1,0:T(8,128)(2,1)} %refs_0_.1, bf16[128,1024]{1,0:T(8,128)(2,1)} %refs_1_.1, bf16[128,1024]{1,0:T(8,128)(2,1)} %refs_2_.1, f32[8,128]{1,0:T(8,128)} %bitcast.4, f32[8,128]{1,0:T(8,128)} %bitcast.5, f32[9,8,128]{2,1,0:T(8,128)} %bitcast.3), custom_call_target="tpu_custom_call" | custom-call | tf_op jit(solution)/shard_map/pallas_call | solution.py:537
  41.3 0.8 %copy.8 = f32[128,1024]{1,0:T(8,128)} copy(f32[128,1024]{1,0:T(8,128)S(1)} %shard_map.64) | data formatting | bytes 1048576

commit v2 on v1

v2 whole, which is shorter than its diff:
```python
import functools

import jax
import jax.numpy as jnp
from jax import lax
from jax.experimental import pallas as pl
from jax.experimental.pallas import tpu as pltpu
from jax.sharding import PartitionSpec as P

MESH = pl.DeviceIdType.MESH
F32 = jnp.float32
BF16 = jnp.bfloat16
NN = (((1,), (0,)), ((), ()))
NT = (((1,), (1,)), ((), ()))
AUX = 16
ROWS = 8
TILE = 16
EPS = 1e-06


def dot(a, b, dims=NN):
    return lax.dot_general(a, b, dims, preferred_element_type=F32)


def split(a):
    high = a.astype(BF16)
    return high, (a - high.astype(F32)).astype(BF16)


def mm(a, b):
    ah, al = a
    bh, bl = b
    return dot(ah, bh) + (dot(ah, bl) + dot(al, bh))


def mm_square(a, b):
    ah, al = a
    bh, bl = b
    right = jnp.concatenate(
        [jnp.concatenate([bh, bl], 1), jnp.concatenate([bh, jnp.zeros_like(bl)], 1)], 0
    )
    both = dot(jnp.concatenate([ah, al], 1), right)
    width = bh.shape[1]
    return both[:, :width] + both[:, width:]


def mm_exact(a, b):
    return dot(jnp.concatenate(a, 1), jnp.concatenate([b, b], 0))


def tile_inverse(low, size):
    lane = lax.broadcasted_iota(jnp.int32, (TILE, size), 1)
    sub = lax.broadcasted_iota(jnp.int32, (TILE, size), 0)
    tile = lane // TILE
    packed = low[:TILE]
    for g in range(1, size // TILE):
        packed = jnp.where(tile == g, low[g * TILE : (g + 1) * TILE], packed)
    inner = lane - tile * TILE
    packed = jnp.where(sub > inner, packed, 0.0)
    x = jnp.where(sub == inner, 1.0, 0.0)
    for c in range(TILE - 1):
        column = jnp.take_along_axis(packed, tile * TILE + c, axis=1)
        x = x - column * x[c : c + 1]
    return jnp.concatenate(
        [jnp.where(tile == g, x, 0.0) for g in range(size // TILE)], 0
    )


def unit_lower_inverse(lowers, size, row, col):
    apart = row ^ col
    inverses = [tile_inverse(low, size) for low in lowers]
    width = TILE
    while width < size:
        mask = (apart >= width) & (apart < 2 * width)
        parts = [split(x) for x in inverses]
        blocks = [split(jnp.where(mask, low, 0.0)) for low in lowers]
        left = [split(mm_square(x, b)) for x, b in zip(parts, blocks)]
        inverses = [x - mm_square(l, p) for x, l, p in zip(inverses, left, parts)]
        width *= 2
    return inverses


def transitions(blocks, size, dim):
    row = lax.broadcasted_iota(jnp.int32, (size, size), 0)
    col = lax.broadcasted_iota(jnp.int32, (size, size), 1)
    aux_row = lax.broadcasted_iota(jnp.int32, (AUX, size), 0)
    staged, lowers = [], []
    for kb, vb, aux in blocks:
        gram = dot(kb, kb, NT)
        norm = jnp.sum(jnp.where(row == col, gram, 0.0), 0, keepdims=True) + EPS
        rk = lax.rsqrt(norm)
        gain = aux[1:2] * (rk * rk)
        decay = aux[0:1]
        cols = jnp.where(aux_row == AUX - 1, gain, aux).T
        lowers.append(jnp.where(row > col, gram * gain, 0.0))
        staged.append((kb, vb, gain, norm * rk / decay, decay[:, size - 1 : size], cols))
    inverses = unit_lower_inverse(lowers, size, row, col)
    eye = (row == col).astype(F32)
    results = []
    for inverse, (kb, vb, gain, unscale, last, cols) in zip(inverses, staged):
        y = mm_exact(split(inverse), kb)
        z = mm_exact(split(inverse * unscale), vb)
        pair = jnp.concatenate([y, z], 1)
        kt = kb.astype(F32).T.astype(BF16)
        moved = dot(
            jnp.concatenate([kt, kt], 1),
            jnp.concatenate(split(pair * cols[:, AUX - 1 : AUX]), 0),
        )
        turn, write = last * (eye - moved[:, :dim]), last * moved[:, dim:]
        results.append((turn, write, pair, cols, gain))
    return results


def local_reads(qb, kb, pair, cols, gain):
    size = qb.shape[0]
    dim = qb.shape[1]
    row = lax.broadcasted_iota(jnp.int32, (size, size), 0)
    col = lax.broadcasted_iota(jnp.int32, (size, size), 1)
    q = qb.astype(F32)
    scale = lax.rsqrt(jnp.sum(q * q, -1, keepdims=True) + EPS) * cols[:, 0:1]
    scores = jnp.where(row >= col, dot(qb, kb, NT) * gain, 0.0)
    seen = mm(split(scores), split(pair))
    return scale * (q - seen[:, :dim]), (scale * cols[:, 2:3]) * seen[:, dim:]


def chain(upper, lower):
    return mm_square(split(upper), split(lower))


def beside(turn, write):
    th, tl = split(turn)
    wh, wl = split(write)
    return jnp.concatenate([th, wh], 1), jnp.concatenate([tl, wl], 1)


def kernel(n_grp, n_seq, heads, *refs):
    q_ref, k_ref, v_ref, f_ref, b_ref, w_ref, out_ref = refs[:7]
    (
        aux,
        kv_out,
        q_out,
        kv_in,
        q_in,
        pairs,
        colb,
        gains,
        turns,
        writes,
        node_t,
        node_w,
        low_t,
        low_w,
        r_out,
        r_in,
        colr,
        near,
        near_in,
        far,
        far_in,
        mid_t,
        mid_w,
        top_t,
        top_w,
    ) = refs[7:32]
    (
        s_kv,
        r_kv,
        s_q,
        r_q,
        s_node,
        r_node,
        s_r,
        r_r,
        s_mid,
        r_mid,
        s_top,
        r_top,
        s_near,
        r_near,
        s_far,
        r_far,
    ) = refs[32:]
    total_bits = (n_grp * n_seq).bit_length() - 1
    middle = list(range(2, total_bits - 2))
    xl, yl = total_bits - 2, total_bits - 1
    n_mid = len(middle)
    size = q_ref.shape[0]
    dim = q_ref.shape[1] // heads
    slots = heads // 2
    waves = slots // 2
    pos = lax.axis_index("grp") * n_seq + lax.axis_index("seq")

    def bit_of(l):
        return (pos // (1 << l)) % 2

    def where_is(number):
        return (number // n_seq, number % n_seq)

    def flipped(*ls):
        return where_is(pos + sum((1 - 2 * bit_of(l)) * (1 << l) for l in ls))

    def columns(i):
        return pl.ds(pl.multiple_of(i * dim, dim), dim)

    def remote(source, target, send, receive, device):
        return pltpu.make_async_remote_copy(
            src_ref=source,
            dst_ref=target,
            send_sem=send,
            recv_sem=receive,
            device_id=device,
            device_id_type=MESH,
        )

    core, zl, xx, yy = bit_of(0), bit_of(1), bit_of(xl), bit_of(yl)
    other = 1 - core
    beside_me, across, diagonal = flipped(0), flipped(1), flipped(0, 1)
    tops = (flipped(xl), flipped(yl), flipped(xl, yl))
    mine = 2 * yy + xx
    theirs = (2 * yy + 1 - xx, 2 * (1 - yy) + xx, 2 * (1 - yy) + 1 - xx)
    greeted = [beside_me, across, diagonal, *tops] + [flipped(l) for l in middle]
    barrier = pltpu.get_barrier_semaphore()
    for device in greeted:
        pl.semaphore_signal(barrier, inc=1, device_id=device, device_id_type=MESH)

    total = f_ref[...]
    lane = lax.broadcasted_iota(jnp.int32, total.shape, 1)
    step = 1
    while step < size:
        total = total + jnp.where(lane >= step, pltpu.roll(total, step, 1), 0.0)
        step *= 2
    decay = jnp.exp(-total)
    aux[...] = jnp.zeros_like(aux)
    levels = w_ref.shape[0]
    for h in range(heads):
        aux[h, 0:1] = decay[h : h + 1]
        aux[h, 1:2] = b_ref[h : h + 1]
        for l in range(levels):
            aux[h, 2 + l : 3 + l] = w_ref[l, h : h + 1]

    for j in range(slots):
        h = other * slots + j
        kv_out[j, :size] = k_ref[:, columns(h)].astype(F32)
        kv_out[j, size : 2 * size] = v_ref[:, columns(h)].astype(F32)
        kv_out[j, 2 * size :] = aux[h]
        q_out[j] = q_ref[:, columns(h)].astype(F32)
    pl.semaphore_wait(barrier, len(greeted))

    pending = []

    def begin(copy):
        copy.start()
        pending.append(copy)
        return copy

    kv_copies = [
        begin(remote(kv_out.at[j], kv_in.at[j], s_kv.at[j], r_kv.at[j], beside_me))
        for j in range(slots)
    ]
    q_copies = [
        begin(remote(q_out.at[j], q_in.at[j], s_q.at[j], r_q.at[j], beside_me))
        for j in range(slots)
    ]

    def own_block(j):
        h = core * slots + j
        return k_ref[:, columns(h)], v_ref[:, columns(h)], aux[h]

    def other_block(j):
        return (
            kv_in[j, :size].astype(BF16),
            kv_in[j, size : 2 * size].astype(BF16),
            kv_in[j, 2 * size :],
        )

    def solve(work):
        done = transitions(
            [own_block(j) if e == 0 else other_block(j) for j, e in work], size, dim
        )
        for (j, e), (turn, write, pair, cols, gain) in zip(work, done):
            s = other if e else core
            turns[s, j] = turn
            writes[s, j] = write
            pairs[e, j] = pair
            colb[e, j] = cols
            gains[e, j] = jnp.broadcast_to(gain, (8, size))

    node_copies = [
        [
            remote(
                source.at[2 * u + 1 - zl],
                target.at[u, zl],
                s_node.at[2 * u + n],
                r_node.at[2 * u + n],
                across,
            )
            for n, (source, target) in enumerate(((node_t, low_t), (node_w, low_w)))
        ]
        for u in range(waves)
    ]
    pending += [copy for copies in node_copies for copy in copies]

    def send_nodes(u):
        for copy in node_copies[u]:
            copy.start()

    def merge(u):
        for j in (2 * u, 2 * u + 1):
            upper = turns[1, j]
            node_t[j] = chain(upper, turns[0, j])
            node_w[j] = chain(upper, writes[0, j]) + writes[1, j]
        low_t[u, zl] = node_t[2 * u + zl]
        low_w[u, zl] = node_w[2 * u + zl]

    def send_mid(m, u, n):
        l = middle[m]
        ref = (mid_t, mid_w)[n].at[m, u, bit_of(l)]
        begin(remote(ref, ref, s_mid.at[m, 2 * u + n], r_mid.at[m, 2 * u + n], flipped(l)))

    def wait_mid(m, u, n):
        l = middle[m]
        ref = (mid_t, mid_w)[n].at[m, u, 1 - bit_of(l)]
        remote(
            ref, ref, s_mid.at[m, 2 * u + n], r_mid.at[m, 2 * u + n], flipped(l)
        ).wait_recv()

    def send_top(u, n):
        ref = (top_t, top_w)[n].at[u, mine]
        for p in range(3):
            i = 4 * p + 2 * u + n
            begin(remote(ref, ref, s_top.at[i], r_top.at[i], tops[p]))

    def wait_top(u, n):
        for p in range(3):
            ref = (top_t, top_w)[n].at[u, theirs[p]]
            i = 4 * p + 2 * u + n
            remote(ref, ref, s_top.at[i], r_top.at[i], tops[p]).wait_recv()

    def lift(m, u, n):
        if m < 0:
            node_copies[u][n].wait_recv()
            ts, ws = low_t.at[u], low_w.at[u]
        else:
            wait_mid(m, u, n)
            ts, ws = mid_t.at[m, u], mid_w.at[m, u]
        value = chain(ts[1], ts[0]) if n == 0 else chain(ts[1], ws[0]) + ws[1]
        if m + 1 < n_mid:
            (mid_t, mid_w)[n][m + 1, u, bit_of(middle[m + 1])] = value
            send_mid(m + 1, u, n)
        else:
            (top_t, top_w)[n][u, mine] = value
            send_top(u, n)

    def reads(group):
        for j in group:
            q_copies[j].wait_recv()
        for j in group:
            h = core * slots + j
            for e in range(2):
                if e == 0:
                    qb, kb = q_ref[:, columns(h)], k_ref[:, columns(h)]
                else:
                    qb, kb = q_in[j].astype(BF16), kv_in[j, :size].astype(BF16)
                s = other if e else core
                r, inside = local_reads(qb, kb, pairs[e, j], colb[e, j], gains[e, j, :1])
                r_out[j, s, :size] = r
                r_out[j, s, size:] = (kv_in[j, 2 * size :] if e else aux[h])[4 : 4 + ROWS]
                near[j, s] = inside
        for j in group:
            seen = mm(split(r_out[j, 1, :size]), beside(turns[0, j], writes[0, j]))
            weight = jnp.where(core == 1, colb[0, j], colb[1, j])[:, 3:4]
            r_out[j, 1, :size] = seen[:, :dim]
            near[j, 1] += weight * seen[:, dim:]

    r_copies = {}

    def send_reads(u):
        j = 2 * u + 1 - zl
        for s in range(2):
            i = 2 * u + s
            r_copies[u, s] = begin(
                remote(r_out.at[j, s], r_in.at[u, zl, s], s_r.at[i], r_r.at[i], across)
            )
            r_in[u, zl, s] = r_out[2 * u + zl, s]

    def read(u, items, lower, l, gate=None, fresh=False):
        rows = jnp.concatenate([r_in[u, z, s, :size] for z, s in items], 0)
        seen = mm(split(rows), lower)
        for n, (z, s) in enumerate(items):
            part = seen[n * size : (n + 1) * size]
            value = colr[u, z, s][:, l - 1 : l] * part[:, dim:]
            if gate is not None:
                value = jnp.where(gate, value, 0.0)
            far[u, z, s] = value if fresh else far[u, z, s] + value
            new = part[:, :dim]
            r_in[u, z, s, :size] = (
                new if gate is None else jnp.where(gate, new, r_in[u, z, s, :size])
            )

    everyone = [(z, s) for z in range(2) for s in range(2)]

    def low_reads(u):
        for s in range(2):
            r_copies[u, s].wait_recv()
        for z, s in everyone:
            colr[u, z, s] = r_in[u, z, s, size:].T
        for s in range(2):
            far[u, 0, s] = jnp.zeros((size, dim), F32)
        read(u, everyone[2:], beside(low_t[u, 0], low_w[u, 0]), 1, fresh=True)

    def mid_reads(u):
        for m, l in enumerate(middle):
            read(u, everyone, beside(mid_t[m, u, 0], mid_w[m, u, 0]), l, bit_of(l) == 1)

    far_copies = []

    def top_reads(u):
        wait_top(u, 0)
        wait_top(u, 1)
        state = chain(top_t[u, 1], top_w[u, 0]) + top_w[u, 1]
        read(u, everyone, beside(top_t[u, 2 * yy], top_w[u, 2 * yy]), xl, xx == 1)
        lower = split(state)
        gate = yy == 1
        for z, s, device in (
            (1 - zl, core, across),
            (1 - zl, other, diagonal),
            (zl, other, beside_me),
            (zl, core, None),
        ):
            seen = mm(split(r_in[u, z, s, :size]), lower)
            weight = colr[u, z, s][:, yl - 1 : yl]
            far[u, z, s] += jnp.where(gate, weight * seen, 0.0)
            h = core * slots + 2 * u + zl
            if device is None:
                far_in[h] = far[u, zl, core]
                continue
            i = 3 * u + len(far_copies) % 3
            far_copies.append(
                begin(remote(far.at[u, z, s], far_in.at[h], s_far.at[i], r_far.at[i], device))
            )

    solve([(0, 0), (1, 0)])
    for j in (0, 1):
        kv_copies[j].wait_recv()
    solve([(0, 1), (1, 1)])
    merge(0)
    send_nodes(0)
    for j in range(2, slots):
        kv_copies[j].wait_recv()
    solve([(j, e) for j in (2, 3) for e in range(2)])
    merge(1)
    send_nodes(1)
    lift(-1, 0, 0)
    lift(-1, 0, 1)
    reads((0, 1))
    reads((2, 3))
    lift(-1, 1, 0)
    lift(-1, 1, 1)
    for u in range(waves):
        send_reads(u)
    near_copies = [
        begin(
            remote(near.at[j, other], near_in.at[j], s_near.at[j], r_near.at[j], beside_me)
        )
        for j in range(slots)
    ]
    for m in range(n_mid - 1):
        for u in range(waves):
            lift(m, u, 0)
            lift(m, u, 1)
    for u in range(waves):
        lift(n_mid - 1, u, 0)
        lift(n_mid - 1, u, 1)
    for u in range(waves):
        low_reads(u)
        mid_reads(u)
        top_reads(u)

    for copy in near_copies:
        copy.wait_recv()
    for u in range(waves):
        for n, (c, z) in enumerate(((core, 1 - zl), (other, 1 - zl), (other, zl), (core, zl))):
            j = 2 * u + z
            h = c * slots + j
            if n < 3:
                i = 3 * u + n
                device = (across, diagonal, beside_me)[n]
                remote(
                    far.at[u, zl, core], far_in.at[h], s_far.at[i], r_far.at[i], device
                ).wait_recv()
            here = near[j, core] if n in (0, 3) else near_in[j]
            out_ref[:, columns(h)] = here + far_in[h]
    for copy in pending:
        copy.wait_send()


def on_device(n_grp, n_seq, queries, keys, values, forget, beta, level_weights):
    size = queries.shape[0]
    heads = forget.shape[1]
    dim = queries.shape[1] // heads
    slots = heads // 2
    n_mid = (n_grp * n_seq).bit_length() - 5
    dma = pltpu.SemaphoreType.DMA

    def vmem(*shape):
        return pltpu.VMEM(shape, F32)

    return pl.pallas_call(
        functools.partial(kernel, n_grp, n_seq, heads),
        out_shape=pltpu.VMEM((size, heads * dim), F32),
        in_specs=[pl.BlockSpec(memory_space=pltpu.VMEM)] * 6,
        out_specs=pl.BlockSpec(memory_space=pltpu.VMEM),
        scratch_shapes=[
            vmem(heads, AUX, size),
            vmem(slots, 2 * size + AUX, dim),
            vmem(slots, size, dim),
            vmem(slots, 2 * size + AUX, dim),
            vmem(slots, size, dim),
            vmem(2, slots, size, 2 * dim),
            vmem(2, slots, size, AUX),
            vmem(2, slots, 8, size),
        ]
        + [vmem(2, slots, dim, dim)] * 2
        + [vmem(slots, dim, dim)] * 2
        + [vmem(2, 2, dim, dim)] * 2
        + [
            vmem(slots, 2, size + ROWS, dim),
            vmem(2, 2, 2, size + ROWS, dim),
            vmem(2, 2, 2, size, ROWS),
            vmem(slots, 2, size, dim),
            vmem(slots, size, dim),
            vmem(2, 2, 2, size, dim),
            vmem(heads, size, dim),
        ]
        + [vmem(n_mid, 2, 2, dim, dim)] * 2
        + [vmem(2, 4, dim, dim)] * 2
        + [dma((slots,))] * 4
        + [dma((4,))] * 4
        + [dma((n_mid, 4))] * 2
        + [dma((12,))] * 2
        + [dma((slots,))] * 2
        + [dma((6,))] * 2,
        compiler_params=pltpu.CompilerParams(collective_id=0, has_side_effects=True),
    )(
        queries,
        keys,
        values,
        forget.T,
        beta.T,
        jnp.transpose(level_weights, (0, 2, 1)),
    )


def solution(mesh):
    both = P(("grp", "seq"), None)
    return jax.shard_map(
        functools.partial(on_device, mesh.shape["grp"], mesh.shape["seq"]),
        mesh=mesh,
        in_specs=(both, both, both, both, both, P(None, ("grp", "seq"), None)),
        out_specs=both,
        check_vma=False,
    )
```

time: 42.3 us -> 39.1 us (0.924)
  Pallas kernels: 41.3 us -> 38.2 us
    pallas_call x1, Pallas kernels: 41.3 us -> 38.2 us  [on_device(): pl.pallas_call(functools.partial(kernel, n_grp, n_seq, heads), out_shape=...]
where the time goes in v2:
time: 39.1 us; the launch traced here: 39 us
  Pallas kernels  38.2 us (98%)
  local copies, waits for them, and re-layouts  0.8 us (2%)
    pallas_call x1, Pallas kernels, on_device(): pl.pallas_call(functools.partial(kernel, n_grp, n_seq, heads), out_shape=...  38.2 us
    unnamed x1, local copies, waits for them, and re-layouts  0.8 us

profile of v2, /device:TPU:0, one launch (start us, length us, event | category | flops | bytes accessed | tf_op | source)
XLA Modules:
  0.0 39.0 jit_solution(4343890831291057617)
XLA Ops:
  0.0 38.2 %shard_map.64 = f32[128,1024]{1,0:T(8,128)S(1)} custom-call(bf16[128,1024]{1,0:T(8,128)(2,1)} %refs_0_.1, bf16[128,1024]{1,0:T(8,128)(2,1)} %refs_1_.1, bf16[128,1024]{1,0:T(8,128)(2,1)} %refs_2_.1, f32[8,128]{1,0:T(8,128)} %bitcast.4, f32[8,128]{1,0:T(8,128)} %bitcast.5, f32[9,8,128]{2,1,0:T(8,128)} %bitcast.3), custom_call_target="tpu_custom_call" | custom-call | tf_op jit(solution)/shard_map/pallas_call | solution.py:508
  38.2 0.8 %copy.8 = f32[128,1024]{1,0:T(8,128)} copy(f32[128,1024]{1,0:T(8,128)S(1)} %shard_map.64) | data formatting | bytes 1048576

commit v3 on v2

--- a/solution.py
+++ b/solution.py
@@ -134,7 +134,7 @@
 
 
 def kernel(n_grp, n_seq, heads, *refs):
-    q_ref, k_ref, v_ref, f_ref, b_ref, w_ref, out_ref = refs[:7]
+    arguments, out_ref = refs[:6], refs[6]
     (
         aux,
         kv_out,
@@ -161,7 +161,9 @@
         mid_w,
         top_t,
         top_w,
-    ) = refs[7:32]
+        *held,
+    ) = refs[7:38]
+    q_ref, k_ref, v_ref, f_ref, b_ref, w_ref = held
     (
         s_kv,
         r_kv,
@@ -179,7 +181,8 @@
         r_near,
         s_far,
         r_far,
-    ) = refs[32:]
+        s_load,
+    ) = refs[38:]
     total_bits = (n_grp * n_seq).bit_length() - 1
     middle = list(range(2, total_bits - 2))
     xl, yl = total_bits - 2, total_bits - 1
@@ -222,6 +225,15 @@
     barrier = pltpu.get_barrier_semaphore()
     for device in greeted:
         pl.semaphore_signal(barrier, inc=1, device_id=device, device_id_type=MESH)
+
+    loads = [
+        pltpu.make_async_copy(source, target, s_load.at[i])
+        for i, (source, target) in enumerate(zip(arguments, held))
+    ]
+    for i in (3, 4, 5, 1, 2, 0):
+        loads[i].start()
+    for i in (3, 4, 5):
+        loads[i].wait()
 
     total = f_ref[...]
     lane = lax.broadcasted_iota(jnp.int32, total.shape, 1)
@@ -238,12 +250,15 @@
         for l in range(levels):
             aux[h, 2 + l : 3 + l] = w_ref[l, h : h + 1]
 
-    for j in range(slots):
+    away = [2 * u + 1 - zl for u in range(waves)]
+    kept = [2 * u + zl for u in range(waves)]
+    loads[1].wait()
+    loads[2].wait()
+    for j in away + kept:
         h = other * slots + j
         kv_out[j, :size] = k_ref[:, columns(h)].astype(F32)
         kv_out[j, size : 2 * size] = v_ref[:, columns(h)].astype(F32)
         kv_out[j, 2 * size :] = aux[h]
-        q_out[j] = q_ref[:, columns(h)].astype(F32)
     pl.semaphore_wait(barrier, len(greeted))
 
     pending = []
@@ -253,14 +268,14 @@
         pending.append(copy)
         return copy
 
-    kv_copies = [
-        begin(remote(kv_out.at[j], kv_in.at[j], s_kv.at[j], r_kv.at[j], beside_me))
-        for j in range(slots)
-    ]
-    q_copies = [
-        begin(remote(q_out.at[j], q_in.at[j], s_q.at[j], r_q.at[j], beside_me))
-        for j in range(slots)
-    ]
+    def kv_copy(j):
+        return remote(kv_out.at[j], kv_in.at[j], s_kv.at[j], r_kv.at[j], beside_me)
+
+    def q_copy(j):
+        return remote(q_out.at[j], q_in.at[j], s_q.at[j], r_q.at[j], beside_me)
+
+    for j in away + kept:
+        begin(kv_copy(j))
 
     def own_block(j):
         h = core * slots + j
@@ -304,13 +319,10 @@
         for copy in node_copies[u]:
             copy.start()
 
-    def merge(u):
-        for j in (2 * u, 2 * u + 1):
-            upper = turns[1, j]
-            node_t[j] = chain(upper, turns[0, j])
-            node_w[j] = chain(upper, writes[0, j]) + writes[1, j]
-        low_t[u, zl] = node_t[2 * u + zl]
-        low_w[u, zl] = node_w[2 * u + zl]
+    def merge(j):
+        upper = turns[1, j]
+        node_t[j] = chain(upper, turns[0, j])
+        node_w[j] = chain(upper, writes[0, j]) + writes[1, j]
 
     def send_mid(m, u, n):
         l = middle[m]
@@ -324,17 +336,34 @@
             ref, ref, s_mid.at[m, 2 * u + n], r_mid.at[m, 2 * u + n], flipped(l)
         ).wait_recv()
 
+    first_x, second_x = xx == 0, xx == 1
+    first_y, second_y = yy == 0, yy == 1
+
+    def top_copy(u, n, p, group):
+        ref = (top_t, top_w)[n].at[u, group]
+        i = 4 * p + 2 * u + n
+        return remote(ref, ref, s_top.at[i], r_top.at[i], tops[p])
+
+    def each_top(u, n, act):
+        def do(*ps):
+            def run():
+                for p in ps:
+                    act(top_copy(u, n, p, mine))
+
+            return run
+
+        if n == 1:
+            pl.when(first_x)(do(0))
+            pl.when(first_y)(do(1, 2))
+        else:
+            pl.when(first_x & second_y)(do(0))
+            pl.when(second_x & first_y)(do(1, 2))
+
     def send_top(u, n):
-        ref = (top_t, top_w)[n].at[u, mine]
-        for p in range(3):
-            i = 4 * p + 2 * u + n
-            begin(remote(ref, ref, s_top.at[i], r_top.at[i], tops[p]))
-
-    def wait_top(u, n):
-        for p in range(3):
-            ref = (top_t, top_w)[n].at[u, theirs[p]]
-            i = 4 * p + 2 * u + n
-            remote(ref, ref, s_top.at[i], r_top.at[i], tops[p]).wait_recv()
+        each_top(u, n, lambda copy: copy.start())
+
+    def wait_top(u, n, p):
+        top_copy(u, n, p, theirs[p]).wait_recv()
 
     def lift(m, u, n):
         if m < 0:
@@ -353,7 +382,7 @@
 
     def reads(group):
         for j in group:
-            q_copies[j].wait_recv()
+            q_copy(j).wait_recv()
         for j in group:
             h = core * slots + j
             for e in range(2):
@@ -383,19 +412,14 @@
             )
             r_in[u, zl, s] = r_out[2 * u + zl, s]
 
-    def read(u, items, lower, l, gate=None, fresh=False):
+    def read(u, items, lower, l, fresh=False):
         rows = jnp.concatenate([r_in[u, z, s, :size] for z, s in items], 0)
         seen = mm(split(rows), lower)
         for n, (z, s) in enumerate(items):
             part = seen[n * size : (n + 1) * size]
             value = colr[u, z, s][:, l - 1 : l] * part[:, dim:]
-            if gate is not None:
-                value = jnp.where(gate, value, 0.0)
             far[u, z, s] = value if fresh else far[u, z, s] + value
-            new = part[:, :dim]
-            r_in[u, z, s, :size] = (
-                new if gate is None else jnp.where(gate, new, r_in[u, z, s, :size])
-            )
+            r_in[u, z, s, :size] = part[:, :dim]
 
     everyone = [(z, s) for z in range(2) for s in range(2)]
 
@@ -410,46 +434,69 @@
 
     def mid_reads(u):
         for m, l in enumerate(middle):
-            read(u, everyone, beside(mid_t[m, u, 0], mid_w[m, u, 0]), l, bit_of(l) == 1)
-
-    far_copies = []
-
-    def top_reads(u):
-        wait_top(u, 0)
-        wait_top(u, 1)
-        state = chain(top_t[u, 1], top_w[u, 0]) + top_w[u, 1]
-        read(u, everyone, beside(top_t[u, 2 * yy], top_w[u, 2 * yy]), xl, xx == 1)
-        lower = split(state)
-        gate = yy == 1
-        for z, s, device in (
+
+            @pl.when(bit_of(l) == 1)
+            def _():
+                read(u, everyone, beside(mid_t[m, u, 0], mid_w[m, u, 0]), l)
+
+    def far_copy(u, n):
+        z, s, device = (
             (1 - zl, core, across),
             (1 - zl, other, diagonal),
             (zl, other, beside_me),
-            (zl, core, None),
-        ):
-            seen = mm(split(r_in[u, z, s, :size]), lower)
-            weight = colr[u, z, s][:, yl - 1 : yl]
-            far[u, z, s] += jnp.where(gate, weight * seen, 0.0)
-            h = core * slots + 2 * u + zl
-            if device is None:
-                far_in[h] = far[u, zl, core]
-                continue
-            i = 3 * u + len(far_copies) % 3
-            far_copies.append(
-                begin(remote(far.at[u, z, s], far_in.at[h], s_far.at[i], r_far.at[i], device))
-            )
-
-    solve([(0, 0), (1, 0)])
-    for j in (0, 1):
-        kv_copies[j].wait_recv()
-    solve([(0, 1), (1, 1)])
-    merge(0)
-    send_nodes(0)
-    for j in range(2, slots):
-        kv_copies[j].wait_recv()
-    solve([(j, e) for j in (2, 3) for e in range(2)])
-    merge(1)
-    send_nodes(1)
+        )[n]
+        h = core * slots + 2 * u + zl
+        i = 3 * u + n
+        return remote(far.at[u, z, s], far_in.at[h], s_far.at[i], r_far.at[i], device)
+
+    def top_reads(u):
+        @pl.when(second_x)
+        def _():
+            wait_top(u, 1, 0)
+            pl.when(second_y)(functools.partial(wait_top, u, 0, 0))
+            read(u, everyone, beside(top_t[u, 2 * yy], top_w[u, 2 * yy]), xl)
+
+        @pl.when(second_y)
+        def _():
+            pl.when(second_x)(functools.partial(wait_top, u, 0, 1))
+            pl.when(first_x)(functools.partial(wait_top, u, 0, 2))
+            wait_top(u, 1, 1)
+            wait_top(u, 1, 2)
+            lower = split(chain(top_t[u, 1], top_w[u, 0]) + top_w[u, 1])
+            for n, (z, s) in enumerate(
+                ((1 - zl, core), (1 - zl, other), (zl, other), (zl, core))
+            ):
+                seen = mm(split(r_in[u, z, s, :size]), lower)
+                far[u, z, s] += colr[u, z, s][:, yl - 1 : yl] * seen
+                if n < 3:
+                    far_copy(u, n).start()
+
+        @pl.when(first_y)
+        def _():
+            for n in range(3):
+                far_copy(u, n).start()
+
+        far_in[core * slots + 2 * u + zl] = far[u, zl, core]
+
+    solve([(j, 0) for j in away])
+    loads[0].wait()
+    for j in range(slots):
+        q_out[j] = q_ref[:, columns(other * slots + j)].astype(F32)
+    for j in range(slots):
+        begin(q_copy(j))
+    for j in away:
+        kv_copy(j).wait_recv()
+    solve([(j, 1) for j in away])
+    for u in range(waves):
+        merge(away[u])
+        send_nodes(u)
+    for j in kept:
+        kv_copy(j).wait_recv()
+    solve([(j, e) for j in kept for e in range(2)])
+    for u in range(waves):
+        merge(kept[u])
+        low_t[u, zl] = node_t[kept[u]]
+        low_w[u, zl] = node_w[kept[u]]
     lift(-1, 0, 0)
     lift(-1, 0, 1)
     reads((0, 1))
@@ -492,6 +539,11 @@
             out_ref[:, columns(h)] = here + far_in[h]
     for copy in pending:
         copy.wait_send()
+    for u in range(waves):
+        for n in range(3):
+            far_copy(u, n).wait_send()
+        for n in range(2):
+            each_top(u, n, lambda copy: copy.wait_send())
 
 
 def on_device(n_grp, n_seq, queries, keys, values, forget, beta, level_weights):
@@ -501,6 +553,8 @@
     slots = heads // 2
     n_mid = (n_grp * n_seq).bit_length() - 5
     dma = pltpu.SemaphoreType.DMA
+    small = forget.T, beta.T, jnp.transpose(level_weights, (0, 2, 1))
+    arguments = (queries, keys, values, *small)
 
     def vmem(*shape):
         return pltpu.VMEM(shape, F32)
@@ -508,7 +562,7 @@
     return pl.pallas_call(
         functools.partial(kernel, n_grp, n_seq, heads),
         out_shape=pltpu.VMEM((size, heads * dim), F32),
-        in_specs=[pl.BlockSpec(memory_space=pltpu.VMEM)] * 6,
+        in_specs=[pl.BlockSpec(memory_space=pl.ANY)] * 6,
         out_specs=pl.BlockSpec(memory_space=pltpu.VMEM),
         scratch_shapes=[
             vmem(heads, AUX, size),
@@ -534,21 +588,15 @@
         ]
         + [vmem(n_mid, 2, 2, dim, dim)] * 2
         + [vmem(2, 4, dim, dim)] * 2
+        + [pltpu.VMEM(a.shape, a.dtype) for a in arguments]
         + [dma((slots,))] * 4
         + [dma((4,))] * 4
         + [dma((n_mid, 4))] * 2
         + [dma((12,))] * 2
         + [dma((slots,))] * 2
-        + [dma((6,))] * 2,
+        + [dma((6,))] * 3,
         compiler_params=pltpu.CompilerParams(collective_id=0, has_side_effects=True),
-    )(
-        queries,
-        keys,
-        values,
-        forget.T,
-        beta.T,
-        jnp.transpose(level_weights, (0, 2, 1)),
-    )
+    )(*arguments)
 
 
 def solution(mesh):

time: 39.1 us -> 36.6 us (0.936)
  the two profiles are of different devices: /device:TPU:0 before, /device:TPU:13 now
where the time goes in v3:
time: 36.6 us; the launch traced here: 36.4 us
  Pallas kernels  35.6 us (97%)
  local copies, waits for them, and re-layouts  0.8 us (2%)
    pallas_call x1, Pallas kernels, on_device(): pl.pallas_call(functools.partial(kernel, n_grp, n_seq, heads), out_shape=...  35.6 us
    unnamed x1, local copies, waits for them, and re-layouts  0.8 us

profile of v3, /device:TPU:13, one launch (start us, length us, event | category | flops | bytes accessed | tf_op | source)
XLA Modules:
  0.0 36.4 jit_solution(11786671042798656422)
XLA Ops:
  0.0 35.6 %shard_map.64 = f32[128,1024]{1,0:T(8,128)S(1)} custom-call(bf16[128,1024]{1,0:T(8,128)(2,1)} %refs_0_.1, bf16[128,1024]{1,0:T(8,128)(2,1)} %refs_1_.1, bf16[128,1024]{1,0:T(8,128)(2,1)} %refs_2_.1, f32[8,128]{1,0:T(8,128)} %bitcast.4, f32[8,128]{1,0:T(8,128)} %bitcast.5, f32[9,8,128]{2,1,0:T(8,128)} %bitcast.3), custom_call_target="tpu_custom_call" | custom-call | tf_op jit(solution)/shard_map/pallas_call | solution.py:562
  35.6 0.8 %copy.8 = f32[128,1024]{1,0:T(8,128)} copy(f32[128,1024]{1,0:T(8,128)S(1)} %shard_map.64) | data formatting | bytes 1048576

commit v4 on v3

--- a/solution.py
+++ b/solution.py
@@ -489,7 +489,10 @@
     solve([(j, 1) for j in away])
     for u in range(waves):
         merge(away[u])
-        send_nodes(u)
+    for n in range(2):
+        node_copies[0][n].start()
+    for n in range(2):
+        node_copies[1][n].start()
     for j in kept:
         kv_copy(j).wait_recv()
     solve([(j, e) for j in kept for e in range(2)])
@@ -501,10 +504,7 @@
     lift(-1, 0, 1)
     reads((0, 1))
     reads((2, 3))
-    lift(-1, 1, 0)
-    lift(-1, 1, 1)
-    for u in range(waves):
-        send_reads(u)
+    send_reads(0)
     near_copies = [
         begin(
             remote(near.at[j, other], near_in.at[j], s_near.at[j], r_near.at[j], beside_me)
@@ -512,12 +512,18 @@
         for j in range(slots)
     ]
     for m in range(n_mid - 1):
-        for u in range(waves):
-            lift(m, u, 0)
-            lift(m, u, 1)
-    for u in range(waves):
-        lift(n_mid - 1, u, 0)
-        lift(n_mid - 1, u, 1)
+        lift(m, 0, 0)
+        lift(m, 0, 1)
+    lift(n_mid - 1, 0, 0)
+    lift(-1, 1, 0)
+    lift(-1, 1, 1)
+    send_reads(1)
+    lift(n_mid - 1, 0, 1)
+    for m in range(n_mid - 1):
+        lift(m, 1, 0)
+        lift(m, 1, 1)
+    lift(n_mid - 1, 1, 0)
+    lift(n_mid - 1, 1, 1)
     for u in range(waves):
         low_reads(u)
         mid_reads(u)

time: 36.6 us -> 35.2 us (0.962)
  the two profiles are of different devices: /device:TPU:13 before, /device:TPU:7 now
where the time goes in v4:
time: 35.2 us; the launch traced here: 35.1 us
  Pallas kernels  34.3 us (97%)
  local copies, waits for them, and re-layouts  0.8 us (2%)
    pallas_call x1, Pallas kernels, on_device(): pl.pallas_call(functools.partial(kernel, n_grp, n_seq, heads), out_shape=...  34.3 us
    unnamed x1, local copies, waits for them, and re-layouts  0.8 us

profile of v4, /device:TPU:7, one launch (start us, length us, event | category | flops | bytes accessed | tf_op | source)
XLA Modules:
  0.0 35.1 jit_solution(15418231973761930961)
XLA Ops:
  0.0 34.3 %shard_map.64 = f32[128,1024]{1,0:T(8,128)S(1)} custom-call(bf16[128,1024]{1,0:T(8,128)(2,1)} %refs_0_.1, bf16[128,1024]{1,0:T(8,128)(2,1)} %refs_1_.1, bf16[128,1024]{1,0:T(8,128)(2,1)} %refs_2_.1, f32[8,128]{1,0:T(8,128)} %bitcast.4, f32[8,128]{1,0:T(8,128)} %bitcast.5, f32[9,8,128]{2,1,0:T(8,128)} %bitcast.3), custom_call_target="tpu_custom_call" | custom-call | tf_op jit(solution)/shard_map/pallas_call | solution.py:568
  34.3 0.8 %copy.8 = f32[128,1024]{1,0:T(8,128)} copy(f32[128,1024]{1,0:T(8,128)S(1)} %shard_map.64) | data formatting | bytes 1048576

commit v5 on v4

--- a/solution.py
+++ b/solution.py
@@ -410,7 +410,11 @@
             r_copies[u, s] = begin(
                 remote(r_out.at[j, s], r_in.at[u, zl, s], s_r.at[i], r_r.at[i], across)
             )
-            r_in[u, zl, s] = r_out[2 * u + zl, s]
+
+    def keep_reads():
+        for u in range(waves):
+            for s in range(2):
+                r_in[u, zl, s] = r_out[kept[u], s]
 
     def read(u, items, lower, l, fresh=False):
         rows = jnp.concatenate([r_in[u, z, s, :size] for z, s in items], 0)
@@ -502,15 +506,8 @@
         low_w[u, zl] = node_w[kept[u]]
     lift(-1, 0, 0)
     lift(-1, 0, 1)
-    reads((0, 1))
-    reads((2, 3))
+    reads(away)
     send_reads(0)
-    near_copies = [
-        begin(
-            remote(near.at[j, other], near_in.at[j], s_near.at[j], r_near.at[j], beside_me)
-        )
-        for j in range(slots)
-    ]
     for m in range(n_mid - 1):
         lift(m, 0, 0)
         lift(m, 0, 1)
@@ -518,6 +515,14 @@
     lift(-1, 1, 0)
     lift(-1, 1, 1)
     send_reads(1)
+    reads(kept)
+    keep_reads()
+    near_copies = [
+        begin(
+            remote(near.at[j, other], near_in.at[j], s_near.at[j], r_near.at[j], beside_me)
+        )
+        for j in range(slots)
+    ]
     lift(n_mid - 1, 0, 1)
     for m in range(n_mid - 1):
         lift(m, 1, 0)
@@ -529,6 +534,11 @@
         mid_reads(u)
         top_reads(u)
 
+    for u in range(waves):
+        for n in range(2):
+            each_top(u, n, lambda copy: copy.wait_send())
+    for copy in pending:
+        copy.wait_send()
     for copy in near_copies:
         copy.wait_recv()
     for u in range(waves):
@@ -543,13 +553,9 @@
                 ).wait_recv()
             here = near[j, core] if n in (0, 3) else near_in[j]
             out_ref[:, columns(h)] = here + far_in[h]
-    for copy in pending:
-        copy.wait_send()
     for u in range(waves):
         for n in range(3):
             far_copy(u, n).wait_send()
-        for n in range(2):
-            each_top(u, n, lambda copy: copy.wait_send())
 
 
 def on_device(n_grp, n_seq, queries, keys, values, forget, beta, level_weights):

time: 35.2 us -> 34.9 us (level)
  the two profiles are of different devices: /device:TPU:7 before, /device:TPU:5 now
where the time goes in v5:
time: 34.9 us; the launch traced here: 34.7 us
  Pallas kernels  33.9 us (97%)
  local copies, waits for them, and re-layouts  0.8 us (2%)
    pallas_call x1, Pallas kernels, on_device(): pl.pallas_call(functools.partial(kernel, n_grp, n_seq, heads), out_shape=...  33.9 us
    unnamed x1, local copies, waits for them, and re-layouts  0.8 us

profile of v5, /device:TPU:5, one launch (start us, length us, event | category | flops | bytes accessed | tf_op | source)
XLA Modules:
  0.0 34.7 jit_solution(7696240735074833158)
XLA Ops:
  0.0 33.9 %shard_map.64 = f32[128,1024]{1,0:T(8,128)S(1)} custom-call(bf16[128,1024]{1,0:T(8,128)(2,1)} %refs_0_.1, bf16[128,1024]{1,0:T(8,128)(2,1)} %refs_1_.1, bf16[128,1024]{1,0:T(8,128)(2,1)} %refs_2_.1, f32[8,128]{1,0:T(8,128)} %bitcast.4, f32[8,128]{1,0:T(8,128)} %bitcast.5, f32[9,8,128]{2,1,0:T(8,128)} %bitcast.3), custom_call_target="tpu_custom_call" | custom-call | tf_op jit(solution)/shard_map/pallas_call | solution.py:574
  33.9 0.8 %copy.8 = f32[128,1024]{1,0:T(8,128)} copy(f32[128,1024]{1,0:T(8,128)S(1)} %shard_map.64) | data formatting | bytes 1048576

commit v6 on v5

--- a/solution.py
+++ b/solution.py
@@ -300,6 +300,7 @@
             colb[e, j] = cols
             gains[e, j] = jnp.broadcast_to(gain, (8, size))
 
+    late = []
     node_copies = [
         [
             remote(
@@ -327,7 +328,13 @@
     def send_mid(m, u, n):
         l = middle[m]
         ref = (mid_t, mid_w)[n].at[m, u, bit_of(l)]
-        begin(remote(ref, ref, s_mid.at[m, 2 * u + n], r_mid.at[m, 2 * u + n], flipped(l)))
+        copy = remote(ref, ref, s_mid.at[m, 2 * u + n], r_mid.at[m, 2 * u + n], flipped(l))
+        if m + 1 < n_mid:
+            begin(copy)
+            return
+        needed = first_x | first_y | (bit_of(l) == 0)
+        pl.when(needed)(copy.start)
+        late.append((needed, copy))
 
     def wait_mid(m, u, n):
         l = middle[m]
@@ -370,15 +377,27 @@
             node_copies[u][n].wait_recv()
             ts, ws = low_t.at[u], low_w.at[u]
         else:
+            ts, ws = mid_t.at[m, u], mid_w.at[m, u]
+
+        def value():
+            return chain(ts[1], ts[0]) if n == 0 else chain(ts[1], ws[0]) + ws[1]
+
+        if m + 1 < n_mid:
+            if m >= 0:
+                wait_mid(m, u, n)
+            (mid_t, mid_w)[n][m + 1, u, bit_of(middle[m + 1])] = value()
+            send_mid(m + 1, u, n)
+            return
+
+        @pl.when(first_x | first_y)
+        def _():
             wait_mid(m, u, n)
-            ts, ws = mid_t.at[m, u], mid_w.at[m, u]
-        value = chain(ts[1], ts[0]) if n == 0 else chain(ts[1], ws[0]) + ws[1]
-        if m + 1 < n_mid:
-            (mid_t, mid_w)[n][m + 1, u, bit_of(middle[m + 1])] = value
-            send_mid(m + 1, u, n)
-        else:
-            (top_t, top_w)[n][u, mine] = value
+            (top_t, top_w)[n][u, mine] = value()
             send_top(u, n)
+
+        @pl.when(second_x & second_y & (bit_of(middle[m]) == 1))
+        def _():
+            wait_mid(m, u, n)
 
     def reads(group):
         for j in group:
@@ -539,6 +558,8 @@
             each_top(u, n, lambda copy: copy.wait_send())
     for copy in pending:
         copy.wait_send()
+    for needed, copy in late:
+        pl.when(needed)(copy.wait_send)
     for copy in near_copies:
         copy.wait_recv()
     for u in range(waves):

time: 34.9 us -> 34.8 us (level)
  no operation moved by 1% of the time
where the time goes in v6:
time: 34.8 us; the launch traced here: 34.6 us
  Pallas kernels  33.8 us (97%)
  local copies, waits for them, and re-layouts  0.8 us (2%)
    pallas_call x1, Pallas kernels, on_device(): pl.pallas_call(functools.partial(kernel, n_grp, n_seq, heads), out_shape=...  33.8 us
    unnamed x1, local copies, waits for them, and re-layouts  0.8 us

profile of v6, /device:TPU:5, one launch (start us, length us, event | category | flops | bytes accessed | tf_op | source)
XLA Modules:
  0.0 34.6 jit_solution(10654032579222957594)
XLA Ops:
  0.0 33.8 %shard_map.64 = f32[128,1024]{1,0:T(8,128)S(1)} custom-call(bf16[128,1024]{1,0:T(8,128)(2,1)} %refs_0_.1, bf16[128,1024]{1,0:T(8,128)(2,1)} %refs_1_.1, bf16[128,1024]{1,0:T(8,128)(2,1)} %refs_2_.1, f32[8,128]{1,0:T(8,128)} %bitcast.4, f32[8,128]{1,0:T(8,128)} %bitcast.5, f32[9,8,128]{2,1,0:T(8,128)} %bitcast.3), custom_call_target="tpu_custom_call" | custom-call | tf_op jit(solution)/shard_map/pallas_call | solution.py:595
  33.8 0.8 %copy.8 = f32[128,1024]{1,0:T(8,128)} copy(f32[128,1024]{1,0:T(8,128)S(1)} %shard_map.64) | data formatting | bytes 1048576
